TPU v7x, 32 devices: a whole 2x2x4 slice. The times are simulated.
32 devices in a mesh: dp: 8 (over y, x, core), tensor: 4 (over z).
Axes of the slice: x: 2, y: 2, z: 4, core: 2. Of those that a mesh axis runs over, the one named last changes fastest.
Arguments:
- hidden: bfloat16 [2048, 28672], P('dp', 'tensor'), may hold values from -6 to 6
- hidden_check: bfloat16 [8, 28672], P(None, 'tensor'), may hold values from -96 to 96
- down_weight: bfloat16 [28672, 8192], P('tensor', 'dp'), may hold values from -0.03125 to 0.03125
- weight_check: bfloat16 [28672, 64], P('tensor', 'dp'), may hold values from -0.40039062 to 0.40039062
Outputs:
- output: bfloat16 [2048, 8192], P('tensor', 'dp')
- row_residual: float32 [2048, 64], P('tensor', 'dp')
- col_residual: float32 [8192], P('dp')
All inputs are finite; a program needn't handle non-finite values.
Results may differ from a plain program's by a relative error of at most 0.001.
Values may be sent and summed in bfloat16 or wider, within the bound.
No kernel may reach another device: no remote copies, remote signals or barrier semaphores. Data moves between devices by JAX's collectives and lax.ppermute only.
A program may use at most 128 MiB of HBM per device.

v0:
```python
import jax
import jax.numpy as jnp
from jax import lax
from jax.sharding import PartitionSpec as P

CHECK_BLOCK = 128


def shards(hidden, hidden_check, down_weight, weight_check):
    total_rows = hidden.shape[0] * lax.axis_size("dp")
    gathered = lax.all_gather(hidden, "dp", axis=0, tiled=True)
    check_part = jnp.dot(gathered, weight_check, preferred_element_type=jnp.float32)
    check_rows = jnp.dot(hidden_check, down_weight, preferred_element_type=jnp.float32)
    check_sum = check_rows.sum(0)
    partial_value = jnp.dot(gathered, down_weight, preferred_element_type=jnp.float32)
    differ_part = check_part - partial_value.reshape(total_rows, -1, CHECK_BLOCK).sum(-1)
    column_part = partial_value.sum(0)
    column_total = lax.psum(check_sum - column_part, "tensor")
    summed, row_differ = (
        lax.psum_scatter(partial_value, "tensor", scatter_dimension=0, tiled=True),
        lax.psum_scatter(differ_part, "tensor", scatter_dimension=0, tiled=True),
    )
    output = summed.astype(jnp.bfloat16)
    row_residual = row_differ * CHECK_BLOCK ** (-0.5)
    col_residual = column_total * total_rows ** (-0.5)
    return (output, row_residual, col_residual)


def solution(mesh):
    placed = (P("dp", "tensor"), P(None, "tensor"), P("tensor", "dp"), P("tensor", "dp"))
    return jax.shard_map(
        shards,
        mesh=mesh,
        in_specs=placed,
        out_specs=(P("tensor", "dp"), P("tensor", "dp"), P("dp")),
        check_vma=False,
    )
```

profile of v0, /device:TPU:0, one launch (start us, length us, event | category | flops | bytes accessed | tf_op | source)
XLA Modules:
  0.0 383.0 jit_solution(15567807515151135576)
XLA Ops:
  7.2 0.0 copy-start
  7.2 0.0 all-gather.2.cloned.1.call-start
  7.2 0.7 all-gather.2.cloned.1.call-update
  7.9 0.0 reduce-scatter.5.cloned.1.call-start
  8.0 147.6 %all-gather.2.cloned.1.call-done = bf16[2048,7168]{1,0:T(8,128)(2,1)} async-done(((bf16[256,7168]{1,0:T(8,128)(2,1)}), bf16[2048,7168]{1,0:T(8,128)(2,1)}) %all-gather.2.cloned.1.call-update) | async-done | bytes 29360144 | tf_op jit(solution)/shard_map/all_gather | solution.py:11
  155.6 39.3 %bitcast_reduce_fusion = (f32[2048,8]{0,1:T(8,128)S(1)}, f32[2048,1024]{0,1:T(8,128)}) fusion(bf16[2048,7168]{1,0:T(8,128)(2,1)} %all-gather.2.cloned.1.call-done, bf16[7168,1024]{1,0:T(8,128)(2,1)} %param.6), kind=kOutput, calls=%fused_computation | convolution fusion | flops 30066851840 | bytes 52494336 | tf_op jit(solution)/shard_map/dot_general | solution.py:15
  194.9 0.0 copy-done
  194.9 0.0 copy-start.1
  194.9 13.9 %convolution_subtract_fusion = f32[2048,8]{0,1:T(8,128)} fusion(f32[2048,8]{0,1:T(8,128)S(1)} %get-tuple-element.6, bf16[2048,7168]{1,0:T(8,128)(2,1)} %all-gather.2.cloned.1.call-done, bf16[7168,8]{0,1:T(8,128)(2,1)S(1)} %copy-done), kind=kOutput, calls=%fused_computation.1 | convolution fusion | flops 234897408 | bytes 29605888 | tf_op jit(solution)/shard_map/dot_general | solution.py:12
  208.8 0.0 reduce-scatter.5.cloned.1.call-update
  208.8 0.2 reduce-scatter.3.cloned.1.call-start
  209.0 0.5 reduce-scatter.3.cloned.1.call-update
  209.5 0.0 copy-done.1
  209.6 7.2 %convolution_reduce_fusion = f32[1024]{0:T(1024)S(1)} fusion(bf16[8,7168]{1,0:T(8,128)(2,1)S(1)} %copy-done.1, bf16[7168,1024]{1,0:T(8,128)(2,1)} %param.6), kind=kOutput, calls=%fused_computation.2 | convolution fusion | flops 117447680 | bytes 14798848 | tf_op jit(solution)/shard_map/dot_general | solution.py:13
  216.7 3.8 reduce_sum.29
  220.6 11.7 %psum.7 = f32[1024]{0:T(1024)S(1)} all-reduce(f32[1024]{0:T(1024)S(1)} %sub.7), channel_id=1, replica_groups=mesh['dp'=8,'tensor'=4] {'tensor'}, use_global_device_ids=true, to_apply=%region_5.0 | all-reduce | flops 1024 | bytes 8192 | tf_op jit(solution)/shard_map/psum | solution.py:18
  232.3 0.6 broadcast_multiply_fusion.1
  232.9 0.0 reduce-scatter.5.cloned.1.call-done
  232.9 1.3 broadcast_multiply_fusion
  234.2 139.2 %reduce-scatter.3.cloned.1.call-done = f32[512,1024]{0,1:T(8,128)} async-done(((f32[2048,1024]{0,1:T(8,128)}), f32[512,1024]{0,1:T(8,128)}) %reduce-scatter.3.cloned.1.call-update) | async-done | bytes 2097168 | tf_op jit(solution)/shard_map/reduce_scatter | solution.py:20
  373.5 1.7 convert_element_type.3
  375.2 1.3 copy.7
  (1 shorter events, 0.0 us)
Async XLA Ops:
  7.2 187.7 %copy-start = (bf16[7168,8]{0,1:T(8,128)(2,1)S(1)}, bf16[7168,8]{0,1:T(8,128)(2,1)}, u32[]{:S(2)}) copy-start(bf16[7168,8]{0,1:T(8,128)(2,1)} %param.7) | copy-start | bytes 344068
  7.2 148.4 %all-gather.2.cloned.1.call-start = ((), (), s32[]{:S(2)}) async-start(), calls=%async_computation.2 | async-start | bytes 33030144 | tf_op jit(solution)/shard_map/all_gather | solution.py:11
  7.9 225.0 %reduce-scatter.5.cloned.1.call-start = ((), (), s32[]{:S(2)}) async-start(), calls=%async_computation.4 | async-start | bytes 81920 | tf_op jit(solution)/shard_map/reduce_scatter | solution.py:21
  194.9 14.7 %copy-start.1 = (bf16[8,7168]{1,0:T(8,128)(2,1)S(1)}, bf16[8,7168]{1,0:T(8,128)(2,1)}, u32[]{:S(2)}) copy-start(bf16[8,7168]{1,0:T(8,128)(2,1)} %param.5) | copy-start | bytes 344068
  208.8 164.6 %reduce-scatter.3.cloned.1.call-start = ((), (), s32[]{:S(2)}) async-start(), calls=%async_computation.3 | async-start | bytes 10485760 | tf_op jit(solution)/shard_map/reduce_scatter | solution.py:20
Sparse Core Ops, SparseCore 0:
  9.9 145.6 all-gather.1
  208.9 19.3 reduce-scatter.4
  230.7 142.7 reduce-scatter.2
where the time goes:
time: 383 us
  waiting for transfers between devices  288 us (75%)
  matrix products  60.4 us (16%)
  between operations  13.8 us (4%)
  blocking collectives  11.7 us (3%)
  other arithmetic  7.48 us (2%)
    all_gather x1, waiting for transfers between devices, shards(): gathered = lax.all_gather(hidden, 'dp', axis=0, tiled=True)  148 us
    reduce_scatter x1, waiting for transfers between devices, shards(): lax.psum_scatter(partial_value, 'tensor', scatter_dimension=0, tiled=True)  139 us
    dot_general x1, matrix products, shards(): jnp.dot(gathered, down_weight, preferred_element_type=jnp.float32)  39.3 us
    dot_general x1, matrix products, shards(): jnp.dot(gathered, weight_check, preferred_element_type=jnp.float32)  13.9 us
    psum x1, blocking collectives, shards(): column_total = lax.psum(check_sum - column_part, 'tensor')  11.7 us
  transfers between devices with their start and end apart: 3, of which 2 were waited for; matrix products, arithmetic and copies ran while one was open for 3% of the time, Pallas kernels for 0%

commit v1 on v0

v1 whole, which is shorter than its diff:
```python
import functools

import jax
import jax.numpy as jnp
from jax import lax
from jax.experimental import pallas as pl
from jax.experimental.pallas import tpu as pltpu
from jax.sharding import PartitionSpec as P


CHECK_BLOCK = 128
SPAN = 173.0
TAG = 16
CHUNK = 64
GRANT = 28 * 2**20


def split3(value):
    high = value.astype(jnp.bfloat16)
    rest = value - high.astype(jnp.float32)
    middle = rest.astype(jnp.bfloat16)
    low = (rest - middle.astype(jnp.float32)).astype(jnp.bfloat16)
    return high, middle, low


def across(left, right):
    return lax.dot_general(left, right, (((1,), (1,)), ((), ())), preferred_element_type=jnp.float32)


def multiply_body(index, single, which, first, later, steps, deep, pieces, *refs):
    table, parts, refs = refs[0], refs[1 : 1 + pieces], refs[1 + pieces :]
    if first:
        source, check, stored, *refs = refs
    else:
        weight, check, before, *refs = refs
    if later:
        refs = refs[4:]
    own, send1, send2, send3, differ, column, *refs = refs
    if first:
        weight, *refs = refs
    total, joined, coded, checks, sems, *refs = refs
    if first:
        (arrivals,) = refs
    sends = (send1, send2, send3)
    step = pl.program_id(0)
    rows = differ.shape[2]
    width = total.shape[1]
    blocks = differ.shape[1]
    used = len(which) * rows
    slots = [table[4 * index + b] for b in which]
    places = [b if single else 0 for b in which]

    @pl.when(step == 0)
    def _():
        total[...] = jnp.zeros_like(total)
        checks[...] = jnp.zeros_like(checks)
        if first:
            for i in range(steps):
                at = pl.ds(i * deep, deep)
                pltpu.make_async_copy(source.at[at], weight.at[at], arrivals.at[i]).start()

    at_depth = pl.ds(pl.multiple_of(step * deep, deep), deep)
    place = 0
    for part in parts:
        joined[place : place + part.shape[0]] = part[...]
        place += part.shape[0]
    if first:
        joined[used : used + stored.shape[0]] = stored[...]
    checks[...] += across(check[...], joined[:used])
    if first:
        pltpu.make_async_copy(source.at[at_depth], weight.at[at_depth], arrivals.at[step]).wait()
    total[...] += jnp.dot(joined[...], weight[at_depth, :], preferred_element_type=jnp.float32)

    @pl.when(step == steps - 1)
    def _():
        part = min(CHUNK, rows)
        line = lax.broadcasted_iota(jnp.int32, (blocks, width), 0)
        lane = lax.broadcasted_iota(jnp.int32, (blocks, width), 1)
        member = jnp.where(lane // CHECK_BLOCK == line, 1.0, 0.0).astype(jnp.bfloat16)
        columns = jnp.zeros((1, width), jnp.float32)
        for i, slot in enumerate(slots):
            base = i * rows

            def survey(n, carry):
                summed, largest = carry
                value = total[pl.ds(pl.multiple_of(base + n * part, part), part), :]
                return (
                    summed + value.sum(0, keepdims=True),
                    jnp.maximum(largest, jnp.abs(value).max(0, keepdims=True)),
                )

            zero = jnp.zeros((1, width), jnp.float32)
            summed, largest = lax.fori_loop(0, rows // part, survey, (zero, zero))
            columns += summed
            wide = min(128, rows)
            for n in range(rows // wide):
                at = slice(base + n * wide, base + (n + 1) * wide)
                high, middle, low = split3(total[at, :])
                sums = across(member, high) + across(member, middle) + across(member, low)
                differ[i, :, n * wide : (n + 1) * wide] = checks[:, at] - sums
            scale = (jnp.maximum(largest, 1e-30) * 1.01).astype(jnp.bfloat16)
            per = SPAN / scale.astype(jnp.float32)

            @pl.when(slot != 0)
            def _():
                def encode(n, carry):
                    value = total[pl.ds(pl.multiple_of(base + n * part, part), part), :]
                    size = jnp.exp(jnp.abs(value) * per - SPAN / 2)
                    coded[i, pl.ds(pl.multiple_of(n * part, part), part), :] = jnp.where(
                        value < 0, -size, size
                    ).astype(jnp.bfloat16)
                    return carry

                lax.fori_loop(0, rows // part, encode, 0)
                terms = split3(differ[i])
                if rows < 256:
                    pad = jnp.zeros((blocks, 256 - rows), jnp.bfloat16)
                    terms = [jnp.concatenate([t, pad], 1) for t in terms]
                fill = [*terms, jnp.zeros((blocks, width - 768), jnp.bfloat16)]
                tag = [jnp.concatenate(fill, 1), jnp.broadcast_to(scale, (TAG - blocks, width))]
                coded[i, pl.ds(rows, TAG), :] = jnp.concatenate(tag, 0)

            @pl.when(slot == 0)
            def _():
                pltpu.make_async_copy(total.at[pl.ds(base, rows)], own.at[places[i]], sems.at[i]).start()

            for s in range(3):

                @pl.when(slot == s + 1)
                def _():
                    pltpu.make_async_copy(coded.at[i], sends[s].at[places[i]], sems.at[i]).start()

        if first:
            columns = total[used : used + stored.shape[0], :].sum(0, keepdims=True) - columns
        else:
            columns = before[...] - columns
        column[...] = columns
        for i, slot in enumerate(slots):

            @pl.when(slot == 0)
            def _():
                pltpu.make_async_copy(total.at[pl.ds(i * rows, rows)], own.at[places[i]], sems.at[i]).wait()

            @pl.when(slot != 0)
            def _():
                pltpu.make_async_copy(coded.at[i], send1.at[places[i]], sems.at[i]).wait()


def multiply(table, index, which, parts, weight, check, before, stored, single, earlier):
    parts = [pltpu.with_memory_space_constraint(p, pltpu.HBM) for p in parts]
    rows, depth = sum(p.shape[0] for p in parts) // len(which), parts[0].shape[1]
    width = weight.shape[1]
    blocks = check.shape[0]
    deep = next(d for d in (1792, 1024, 512, 256, 128) if depth % d == 0)
    steps = depth // deep
    count = 2 if single else 1
    first = stored is not None
    thin = pl.BlockSpec((blocks, deep), lambda k, s: (0, k))
    anywhere = pl.BlockSpec(memory_space=pl.ANY)
    inside = pl.BlockSpec(memory_space=pltpu.VMEM)
    in_specs = [pl.BlockSpec((p.shape[0], deep), lambda k, s: (0, k)) for p in parts]
    coded = jax.ShapeDtypeStruct((count, rows + TAG, width), jnp.bfloat16)
    out_specs = [
        anywhere,
        anywhere,
        anywhere,
        anywhere,
        pl.BlockSpec((len(which), blocks, rows), lambda k, s: (0, 0, 0)),
        pl.BlockSpec((1, width), lambda k, s: (0, 0)),
    ]
    out_shape = [
        jax.ShapeDtypeStruct((count, rows, width), jnp.float32),
        coded,
        coded,
        coded,
        jax.ShapeDtypeStruct((len(which), blocks, rows), jnp.float32),
        jax.ShapeDtypeStruct((1, width), jnp.float32),
    ]
    tall = len(which) * rows + (16 if first else 0)
    scratch = [
        pltpu.VMEM((tall, width), jnp.float32),
        pltpu.VMEM((tall, deep), jnp.bfloat16),
        pltpu.VMEM((len(which), rows + TAG, width), jnp.bfloat16),
        pltpu.VMEM((blocks, len(which) * rows), jnp.float32),
        pltpu.SemaphoreType.DMA((2,)),
    ]
    if first:
        in_specs += [anywhere, thin, pl.BlockSpec((stored.shape[0], deep), lambda k, s: (0, k))]
        operands = [table, *parts, weight, check, stored]
        out_specs.append(inside)
        out_shape.append(pltpu.VMEM(weight.shape, weight.dtype))
        scratch.append(pltpu.SemaphoreType.DMA((steps,)))
    else:
        in_specs += [inside, thin, pl.BlockSpec((1, width), lambda k, s: (0, 0))]
        operands = [table, *parts, weight, check, before]
    aliases = {}
    if earlier:
        aliases = {len(operands) + i: i for i in range(4)}
        operands += earlier
        in_specs += [anywhere] * 4
    return pl.pallas_call(
        functools.partial(
            multiply_body, index, single, which, first, bool(earlier), steps, deep, len(parts)
        ),
        grid_spec=pltpu.PrefetchScalarGridSpec(
            num_scalar_prefetch=1,
            grid=(steps,),
            in_specs=in_specs,
            out_specs=out_specs,
            scratch_shapes=scratch,
        ),
        out_shape=out_shape,
        input_output_aliases=aliases,
        cost_estimate=pl.CostEstimate(
            flops=2 * len(which) * rows * depth * width,
            bytes_accessed=2 * len(which) * depth * rows,
            transcendentals=0,
        ),
        compiler_params=pltpu.CompilerParams(
            dimension_semantics=("arbitrary",), vmem_limit_bytes=GRANT
        ),
    )(*operands)


def finish_body(index, single, aliased, *refs):
    table, own, get1, get2, get3, differ, differ2 = refs[:7]
    out, row, held, taken, done, sems = refs[8:] if aliased else refs[7:]
    rows, _ = held.shape
    blocks = differ.shape[1]
    part = min(CHUNK, rows)
    gets = (get1, get2, get3)
    marks = [table[4 * index + i] for i in range(4)]
    row[...] = jnp.zeros_like(row)
    for b in range(2):
        place = b if single else 0

        @pl.when(marks[b] == 0)
        def _():
            copies = [pltpu.make_async_copy(own.at[place], held, sems.at[0])]
            for s in range(3):
                copies.append(pltpu.make_async_copy(gets[s].at[place], taken.at[s], sems.at[s + 1]))
            for copy in copies:
                copy.start()
            for copy in copies:
                copy.wait()
            scales = [taken[s, pl.ds(rows, TAG), :][blocks : blocks + 1].astype(jnp.float32) / SPAN for s in range(3)]

            def decode(i, carry):
                at = pl.ds(pl.multiple_of(i * part, part), part)
                value = held[at, :]
                for s in range(3):
                    code = taken[s, at, :].astype(jnp.float32)
                    size = (jnp.log(jnp.abs(code)) + SPAN / 2) * scales[s]
                    value += jnp.where(code < 0, -size, size)
                done[at, :] = value.astype(jnp.bfloat16)
                return carry

            lax.fori_loop(0, rows // part, decode, 0)
            put = pltpu.make_async_copy(
                done, out.at[pl.ds(pl.multiple_of(marks[2 + b], CHUNK), rows), :], sems.at[0]
            )
            put.start()
            whole = differ2[0] if b else differ[0]
            for s in range(3):
                tag = taken[s, pl.ds(rows, TAG), :][:blocks].astype(jnp.float32)
                for j in range(3):
                    whole += tag[:, j * 256 : j * 256 + rows]
            row[b] = whole
            put.wait()


def finish(table, index, own, gets, differ, out, total_rows, single):
    rows, width = own.shape[1:]
    blocks = differ[0].shape[1]
    anywhere = pl.BlockSpec(memory_space=pl.ANY)
    aliased = out is not None
    operands = [table, own, *gets, differ[0], differ[-1]]
    last = differ[-1].shape[0] - 1
    in_specs = [anywhere] * 4 + [
        pl.BlockSpec((1, blocks, rows), lambda i, s: (0, 0, 0)),
        pl.BlockSpec((1, blocks, rows), lambda i, s: (last, 0, 0)),
    ]
    if aliased:
        operands.append(out)
        in_specs.append(anywhere)
    return pl.pallas_call(
        functools.partial(finish_body, index, single, aliased),
        grid_spec=pltpu.PrefetchScalarGridSpec(
            num_scalar_prefetch=1,
            grid=(1,),
            in_specs=in_specs,
            out_specs=[anywhere, pl.BlockSpec((2, blocks, rows), lambda i, s: (0, 0, 0))],
            scratch_shapes=[
                pltpu.VMEM((rows, width), jnp.float32),
                pltpu.VMEM((3, rows + TAG, width), jnp.bfloat16),
                pltpu.VMEM((rows, width), jnp.bfloat16),
                pltpu.SemaphoreType.DMA((4,)),
            ],
        ),
        out_shape=[
            jax.ShapeDtypeStruct((total_rows, width), jnp.bfloat16),
            jax.ShapeDtypeStruct((2, blocks, rows), jnp.float32),
        ],
        input_output_aliases={7: 0} if aliased else {},
        compiler_params=pltpu.CompilerParams(vmem_limit_bytes=GRANT // 2),
        cost_estimate=pl.CostEstimate(flops=0, bytes_accessed=10 * rows * width, transcendentals=0),
    )(*operands)


def planned(mesh_shape, hidden, hidden_check, down_weight, weight_check):
    lanes, chips = mesh_shape["dp"], mesh_shape["tensor"]
    half = hidden.shape[0]
    total_rows = half * lanes
    cut, quarter = half // 2, half // 4
    plan = (
        ("own", (0,), 0, 0),
        ("0a", (1, 2), 0, 0),
        ("0b", (1, 2), 0, cut),
        ("da", (3,), 1, 0),
        ("db", (3,), 1, cut),
        ("1a", (1, 2), 1, 0),
        ("1b", (1, 2), 1, cut),
        ("1c", (1, 2), 1, cut + quarter),
    )
    me, z = lax.axis_index("dp"), lax.axis_index("tensor")
    core, here = me % 2, (me // 2) ^ z
    entries = []
    for _, kinds, other, at in plan:
        direct, swapped = kinds[0], kinds[-1]
        if direct != swapped:
            direct, swapped = jnp.where(core == 0, direct, swapped), jnp.where(core == 0, swapped, direct)
        side = core ^ other
        entries += [here ^ direct, here ^ swapped, side * half + at, (1 - side) * half + at]
    table = jnp.stack([jnp.asarray(e, jnp.int32) for e in entries])
    check = weight_check.T

    def swap(value):
        return lax.ppermute(value, "dp", [(i, i ^ 1) for i in range(lanes)])

    def mix(value):
        return lax.ppermute(value, "dp", [(i, i ^ (4 if i % 2 else 2)) for i in range(lanes)])

    def along(value, kinds, s):
        pairs = []
        for i in range(lanes):
            for kind in kinds:
                target = (i // 2) ^ kind
                pairs.append((i * chips + (target ^ s), i * chips + target))
        return lax.ppermute(value, ("dp", "tensor"), pairs)

    held = {}
    state = {"out": None, "column": None, "weight": down_weight}

    def group(index, parts, stored=None, which=(0, 1)):
        _, kinds = plan[index][:2]
        single = len(kinds) == 1
        earlier, differ = held.pop(index, (None, []))[:2]
        made = multiply(
            table, index, which, parts, state["weight"], check, state["column"], stored, single, earlier
        )
        sent, more, state["column"] = made[:4], made[4], made[5]
        if stored is not None:
            state["weight"] = pltpu.with_memory_space_constraint(made[6], pltpu.VMEM)
        differ = [*differ, more]
        if which[-1] == 0:
            held[index] = sent, differ
            return
        own, *sends = sent
        gets = [along(v, kinds, s + 1) for s, v in enumerate(sends)]
        held[index] = own, gets, differ, single

    def close(index):
        own, gets, differ, single = held[index]
        state["out"], row = finish(
            table, index, own, gets, differ, state["out"], total_rows // chips, single
        )
        return row

    part_a = hidden[:cut]
    hidden, part_a = lax.optimization_barrier((hidden, part_a))
    part_b = hidden[cut:]
    m0a = mix(part_a)
    pa = swap(part_a)
    m0b = mix(part_b)
    pb = swap(part_b)
    group(0, [part_a, part_b], hidden_check, which=(0,))
    group(0, [pa, pb], which=(1,))
    s0a = swap(m0a)
    d0a = mix(s0a)
    group(1, [m0a, s0a])
    s0b = swap(m0b)
    d0b = mix(s0b)
    m1a = mix(pa)
    m1b = mix(pb[:quarter])
    m1c = mix(pb[quarter:])
    group(2, [m0b, s0b])
    group(3, [d0a, swap(d0a)])
    group(4, [d0b, swap(d0b)])
    group(5, [m1a, swap(m1a)])
    r_own, r0a, r0b = close(0), close(1), close(2)
    group(6, [m1b, swap(m1b)])
    group(7, [m1c, swap(m1c)])
    rda, rdb = close(3), close(4)
    columns = state["column"]
    summed = columns
    for s in range(1, chips):
        summed += lax.ppermute(columns, "tensor", [(i, i ^ s) for i in range(chips)])
    r1a, r1b, r1c = close(5), close(6), close(7)

    join = functools.partial(jnp.concatenate, axis=1)
    same = r_own[0] + join([r0a[0], r0b[0]]) + join([rda[1], rdb[1]]) + join([r1a[1], r1b[1], r1c[1]])
    other = r_own[1] + join([r0a[1], r0b[1]]) + join([rda[0], rdb[0]]) + join([r1a[0], r1b[0], r1c[0]])
    row = jnp.where(core == 0, join([same, other]), join([other, same]))
    row_residual = row.T * CHECK_BLOCK ** (-0.5)
    col_residual = summed[0] * total_rows ** (-0.5)
    return state["out"], row_residual, col_residual


def plain(hidden, hidden_check, down_weight, weight_check):
    total_rows = hidden.shape[0] * lax.axis_size("dp")
    gathered = lax.all_gather(hidden, "dp", axis=0, tiled=True)
    check_part = jnp.dot(gathered, weight_check, preferred_element_type=jnp.float32)
    check_rows = jnp.dot(hidden_check, down_weight, preferred_element_type=jnp.float32)
    partial_value = jnp.dot(gathered, down_weight, preferred_element_type=jnp.float32)
    differ_part = check_part - partial_value.reshape(total_rows, -1, CHECK_BLOCK).sum(-1)
    column_total = lax.psum(check_rows.sum(0) - partial_value.sum(0), "tensor")
    summed = lax.psum_scatter(partial_value, "tensor", scatter_dimension=0, tiled=True)
    row_differ = lax.psum_scatter(differ_part, "tensor", scatter_dimension=0, tiled=True)
    return (
        summed.astype(jnp.bfloat16),
        row_differ * CHECK_BLOCK ** (-0.5),
        column_total * total_rows ** (-0.5),
    )


def solution(mesh):
    placed = (P("dp", "tensor"), P(None, "tensor"), P("tensor", "dp"), P("tensor", "dp"))
    shape = dict(mesh.shape)
    square = shape["tensor"] == 4 and shape["dp"] == 2 * shape["tensor"]
    body = functools.partial(planned, shape) if square else plain
    return jax.shard_map(
        body,
        mesh=mesh,
        in_specs=placed,
        out_specs=(P("tensor", "dp"), P("tensor", "dp"), P("dp")),
        check_vma=False,
    )
```

time: 383 us -> 349 us (0.911)
  the two profiles are of different devices: /device:TPU:0 before, /device:TPU:15 now
where the time goes in v1:
time: 349 us; the launch traced here: 348 us
  waiting for transfers between devices  137 us (39%)
  starting transfers between devices  114 us (33%)
  Pallas kernels  90.3 us (26%)
  local copies, waits for them, and re-layouts  3.76 us (1%)
    ppermute x24, starting transfers between devices, along(): return lax.ppermute(value, ('dp', 'tensor'), pairs)  96.8 us
    ppermute x7, waiting for transfers between devices, mix(): lax.ppermute(value, 'dp', [(i, i ^ (4 if i % 2 else 2)) for i in range(la...  86.3 us
    pallas_call x9, Pallas kernels, multiply(): pl.pallas_call(functools.partial(multiply_body, index, single, which, fir...  78 us
    ppermute x24, waiting for transfers between devices, along(): return lax.ppermute(value, ('dp', 'tensor'), pairs)  39.3 us
    pallas_call x8, Pallas kernels, finish(): pl.pallas_call(functools.partial(finish_body, index, single, aliased), gr...  12.3 us
    ppermute x9, starting transfers between devices, swap(): return lax.ppermute(value, 'dp', [(i, i ^ 1) for i in range(lanes)])  11.1 us
    ppermute x3, waiting for transfers between devices, planned(): lax.ppermute(columns, 'tensor', [(i, i ^ s) for i in range(chips)])  7.37 us
  transfers between devices with their start and end apart: 43, of which 14 were waited for; matrix products, arithmetic and copies ran while one was open for 0% of the time, Pallas kernels for 25%

profile of v1, /device:TPU:15, one launch (start us, length us, event | category | flops | bytes accessed | tf_op | source)
XLA Modules:
  0.0 348.5 jit_solution(16293349745709597017)
XLA Ops:
  5.4 19.4 %collective-permute-done.12.refs_1_ = bf16[128,7168]{1,0:T(8,128)(2,1)S(1)} collective-permute-done((bf16[128,7168]{1,0:T(8,128)(2,1)S(1)}, bf16[128,7168]{1,0:T(8,128)(2,1)S(1)}, u32[]{:S(2)}, u32[]{:S(2)}) %collective-permute-start.12) | collective-permute-done | bytes 1835040 | tf_op jit(solution)/shard_map/ppermute | solution.py:341
  26.4 18.1 %collective-permute-done.8.refs_1_ = bf16[128,7168]{1,0:T(8,128)(2,1)S(1)} collective-permute-done((bf16[128,7168]{1,0:T(8,128)(2,1)S(1)}, bf16[128,7168]{1,0:T(8,128)(2,1)S(1)}, u32[]{:S(2)}, u32[]{:S(2)}) %collective-permute-start.8) | collective-permute-done | bytes 1835040 | tf_op jit(solution)/shard_map/ppermute | solution.py:341
  55.0 33.4 %collective-permute-done.14.refs_1_ = bf16[128,7168]{1,0:T(8,128)(2,1)} collective-permute-done((bf16[128,7168]{1,0:T(8,128)(2,1)}, bf16[128,7168]{1,0:T(8,128)(2,1)}, u32[]{:S(2)}, u32[]{:S(2)}) %collective-permute-start.14) | collective-permute-done | bytes 1835040 | tf_op jit(solution)/shard_map/ppermute | solution.py:341
  89.8 11.9 %shard_map.67 = (f32[2,256,1024]{2,1,0:T(8,128)S(1)}, bf16[2,272,1024]{2,1,0:T(8,128)(2,1)S(1)}, bf16[2,272,1024]{2,1,0:T(8,128)(2,1)S(1)}, bf16[2,272,1024]{2,1...) custom-call(s32[32]{0:T(128)S(1)} %stack.77.refs_0_, ...), custom_call_target="tpu_custom_call" | custom-call | flops 3758096384 | bytes 3670016 | tf_op jit(solution)/shard_map/pallas_call | solution.py:201
  101.7 8.5 %shard_map.68 = (f32[2,256,1024]{2,1,0:T(8,128)S(1)}, bf16[2,272,1024]{2,1,0:T(8,128)(2,1)S(1)}, bf16[2,272,1024]{2,1,0:T(8,128)(2,1)S(1)}, bf16[2,272,1024]{2,1...) custom-call(s32[32]{0:T(128)S(1)} %stack.77.refs_0_, ...), custom_call_target="tpu_custom_call", output_to_operand_aliasing={{0}: (6, {}), {1}: (7, {}), {2}: (8, {}), {3}: (9, {})} | custom-call | flops 3758096384 | bytes 3670016 | tf_op jit(solution)/shard_map/pallas_call | solution.py:201
  110.2 7.6 %collective-permute-done.3.refs_1_ = bf16[64,7168]{1,0:T(8,128)(2,1)S(1)} collective-permute-done((bf16[64,7168]{1,0:T(8,128)(2,1)S(1)}, bf16[64,7168]{1,0:T(8,128)(2,1)S(1)}, u32[]{:S(2)}, u32[]{:S(2)}) %collective-permute-start.3) | collective-permute-done | bytes 917536 | tf_op jit(solution)/shard_map/ppermute | solution.py:341
  120.0 7.7 %collective-permute-done.1.refs_1_ = bf16[64,7168]{1,0:T(8,128)(2,1)S(1)} collective-permute-done((bf16[64,7168]{1,0:T(8,128)(2,1)S(1)}, bf16[64,7168]{1,0:T(8,128)(2,1)S(1)}, u32[]{:S(2)}, u32[]{:S(2)}) %collective-permute-start.1) | collective-permute-done | bytes 917536 | tf_op jit(solution)/shard_map/ppermute | solution.py:341
  127.6 4.3 %collective-permute-start.38 = (bf16[2,272,1024]{2,1,0:T(8,128)(2,1)S(1)}, bf16[2,272,1024]{2,1,0:T(8,128)(2,1)S(1)}, u32[]{:S(2)}, u32[]{:S(2)}) collective-permute-start(bf16[2,272,1024]{2,1,0:T(8,128)(2,1)S(1)} %get-tuple-element.128), channel_id=1, source_target_pairs={{2,0},{6,4},{11,9},{15,13},{16,18},{20,22},{25,27},{29,31}} | collective-permute-start | bytes 3342344 | tf_op jit(solution)/shard_map/ppermute | solution.py:349
  134.5 8.9 %shard_map.69 = (f32[1,128,1024]{2,1,0:T(8,128)S(1)}, bf16[1,144,1024]{2,1,0:T(8,128)(2,1)S(1)}, bf16[1,144,1024]{2,1,0:T(8,128)(2,1)S(1)}, bf16[1,144,1024]{2,1...) custom-call(s32[32]{0:T(128)S(1)} %stack.77.refs_0_, bf16[128,7168]{1,0:T(8,128)(2,1)} %copy-done.7, ...), custom_call_target="tpu_custom_call" | custom-call | flops 3758096384 | bytes 3670016 | tf_op jit(solution)/shard_map/pallas_call | solution.py:201
  143.5 11.0 %collective-permute-done.38.refs_3_ = bf16[2,272,1024]{2,1,0:T(8,128)(2,1)S(1)} collective-permute-done((bf16[2,272,1024]{2,1,0:T(8,128)(2,1)S(1)}, bf16[2,272,1024]{2,1,0:T(8,128)(2,1)S(1)}, u32[]{:S(2)}, u32[]{:S(2)}) %collective-permute-start.38) | collective-permute-done | bytes 1114144 | tf_op jit(solution)/shard_map/ppermute | solution.py:349
  156.7 8.9 %shard_map.70 = (f32[1,128,1024]{2,1,0:T(8,128)S(1)}, bf16[1,144,1024]{2,1,0:T(8,128)(2,1)S(1)}, bf16[1,144,1024]{2,1,0:T(8,128)(2,1)S(1)}, bf16[1,144,1024]{2,1...) custom-call(s32[32]{0:T(128)S(1)} %stack.77.refs_0_, bf16[128,7168]{1,0:T(8,128)(2,1)} %copy-done.6, ...), custom_call_target="tpu_custom_call" | custom-call | flops 3758096384 | bytes 3670016 | tf_op jit(solution)/shard_map/pallas_call | solution.py:201
  165.7 9.1 %shard_map.71 = (f32[2,128,1024]{2,1,0:T(8,128)S(1)}, bf16[2,144,1024]{2,1,0:T(8,128)(2,1)S(1)}, bf16[2,144,1024]{2,1,0:T(8,128)(2,1)S(1)}, bf16[2,144,1024]{2,1...) custom-call(s32[32]{0:T(128)S(1)} %stack.77.refs_0_, ...), custom_call_target="tpu_custom_call" | custom-call | flops 3758096384 | bytes 3670016 | tf_op jit(solution)/shard_map/pallas_call | solution.py:201
  176.1 9.1 %shard_map.72 = (f32[2,128,1024]{2,1,0:T(8,128)S(1)}, bf16[2,144,1024]{2,1,0:T(8,128)(2,1)S(1)}, bf16[2,144,1024]{2,1,0:T(8,128)(2,1)S(1)}, bf16[2,144,1024]{2,1...) custom-call(s32[32]{0:T(128)S(1)} %stack.77.refs_0_, ...), custom_call_target="tpu_custom_call" | custom-call | flops 3758096384 | bytes 3670016 | tf_op jit(solution)/shard_map/pallas_call | solution.py:201
  186.5 26.1 %collective-permute-start.36 = (bf16[1,144,1024]{2,1,0:T(8,128)(2,1)S(1)}, bf16[1,144,1024]{2,1,0:T(8,128)(2,1)S(1)}, u32[]{:S(2)}, u32[]{:S(2)}) collective-permute-start(bf16[1,144,1024]{2,1,0:T(8,128)(2,1)S(1)} %get-tuple-element.124), channel_id=1, source_target_pairs={{2,1},{1,2},{6,5},{5,6},{11,8},{8,11},{15,12},{12,15},{16,19},{19,... | collective-permute-start | bytes 884744 | tf_op jit(solution)/shard_map/ppermute | solution.py:349
  215.3 5.0 %collective-permute-start.28 = (bf16[2,144,1024]{2,1,0:T(8,128)(2,1)S(1)}, bf16[2,144,1024]{2,1,0:T(8,128)(2,1)S(1)}, u32[]{:S(2)}, u32[]{:S(2)}) collective-permute-start(bf16[2,144,1024]{2,1,0:T(8,128)(2,1)S(1)} %get-tuple-element.112), channel_id=1, source_target_pairs={{2,3},{6,7},{11,10},{15,14},{16,17},{20,21},{25,24},{29,28}} | collective-permute-start | bytes 1769480 | tf_op jit(solution)/shard_map/ppermute | solution.py:349
  220.3 8.9 %shard_map.73 = (f32[1,128,1024]{2,1,0:T(8,128)S(1)}, bf16[1,144,1024]{2,1,0:T(8,128)(2,1)S(1)}, bf16[1,144,1024]{2,1,0:T(8,128)(2,1)S(1)}, bf16[1,144,1024]{2,1...) custom-call(s32[32]{0:T(128)S(1)} %stack.77.refs_0_, ...), custom_call_target="tpu_custom_call" | custom-call | flops 3758096384 | bytes 3670016 | tf_op jit(solution)/shard_map/pallas_call | solution.py:201
  231.4 6.3 %shard_map.74 = (f32[1,64,1024]{2,1,0:T(8,128)S(1)}, bf16[1,80,1024]{2,1,0:T(8,128)(2,1)S(1)}, bf16[1,80,1024]{2,1,0:T(8,128)(2,1)S(1)}, bf16[1,80,1024]{2,1,0:T...) custom-call(s32[32]{0:T(128)S(1)} %stack.77.refs_0_, bf16[64,7168]{1,0:T(8,128)(2,1)} %copy-done.10, ...), custom_call_target="tpu_custom_call" | custom-call | flops 1879048192 | bytes 1835008 | tf_op jit(solution)/shard_map/pallas_call | solution.py:201
  240.4 3.4 collective-permute-start.24
  243.8 6.3 %shard_map.75 = (f32[1,64,1024]{2,1,0:T(8,128)S(1)}, bf16[1,80,1024]{2,1,0:T(8,128)(2,1)S(1)}, bf16[1,80,1024]{2,1,0:T(8,128)(2,1)S(1)}, bf16[1,80,1024]{2,1,0:T...) custom-call(s32[32]{0:T(128)S(1)} %stack.77.refs_0_, bf16[64,7168]{1,0:T(8,128)(2,1)} %copy-done.11, ...), custom_call_target="tpu_custom_call" | custom-call | flops 1879048192 | bytes 1835008 | tf_op jit(solution)/shard_map/pallas_call | solution.py:201
  254.1 3.3 collective-permute-done.41
  261.1 4.8 %collective-permute-done.19.refs_2_ = bf16[1,80,1024]{2,1,0:T(8,128)(2,1)S(1)} collective-permute-done((bf16[1,80,1024]{2,1,0:T(8,128)(2,1)S(1)}, bf16[1,80,1024]{2,1,0:T(8,128)(2,1)S(1)}, u32[]{:S(2)}, u32[]{:S(2)}) %collective-permute-start.19) | collective-permute-done | bytes 163872 | tf_op jit(solution)/shard_map/ppermute | solution.py:349
  277.5 33.9 %collective-permute-start.21 = (bf16[1,80,1024]{2,1,0:T(8,128)(2,1)S(1)}, bf16[1,80,1024]{2,1,0:T(8,128)(2,1)S(1)}, u32[]{:S(2)}, u32[]{:S(2)}) collective-permute-start(bf16[1,80,1024]{2,1,0:T(8,128)(2,1)S(1)} %get-tuple-element.99), channel_id=1, source_target_pairs={{2,1},{1,2},{6,5},{5,6},{11,8},{8,11},{15,12},{12,15},{16,19},{19,... | collective-permute-start | bytes 491528 | tf_op jit(solution)/shard_map/ppermute | solution.py:349
  311.5 20.4 %collective-permute-done.25.refs_2_ = bf16[2,144,1024]{2,1,0:T(8,128)(2,1)S(1)} collective-permute-done((bf16[2,144,1024]{2,1,0:T(8,128)(2,1)S(1)}, bf16[2,144,1024]{2,1,0:T(8,128)(2,1)S(1)}, u32[]{:S(2)}, u32[]{:S(2)}) %collective-permute-start.25) | collective-permute-done | bytes 589856 | tf_op jit(solution)/shard_map/ppermute | solution.py:349
  342.5 3.1 collective-permute-done.18.refs_4_
  (114 shorter events, 67.6 us)
Async XLA Ops:
  3.4 41.1 %collective-permute-start.8 = (bf16[128,7168]{1,0:T(8,128)(2,1)S(1)}, bf16[128,7168]{1,0:T(8,128)(2,1)S(1)}, u32[]{:S(2)}, u32[]{:S(2)}) collective-permute-start(bf16[128,7168]{1,0:T(8,128)(2,1)S(1)} %slice.61.refs_2_), channel_id=1, source_target_pairs={{0,8},{4,20},{8,0},{12,28},{16,24},{20,4},{24,16},{28,12},{1,9},{5... | collective-permute-start | bytes 5505032 | tf_op jit(solution)/shard_map/ppermute | solution.py:341
  4.2 41.9 %collective-permute-start.5 = (bf16[128,7168]{1,0:T(8,128)(2,1)S(1)}, bf16[128,7168]{1,0:T(8,128)(2,1)}, u32[]{:S(2)}, u32[]{:S(2)}) collective-permute-start(bf16[128,7168]{1,0:T(8,128)(2,1)S(1)} %slice.60.refs_1_), channel_id=1, source_target_pairs={{0,4},{4,0},{8,12},{12,8},{16,20},{20,16},{24,28},{28,24},{1,5},{5... | collective-permute-start | bytes 5505032 | tf_op jit(solution)/shard_map/ppermute | solution.py:338
  46.1 85.9 %collective-permute-start.6 = (bf16[128,7168]{1,0:T(8,128)(2,1)}, bf16[128,7168]{1,0:T(8,128)(2,1)}, u32[]{:S(2)}, u32[]{:S(2)}) collective-permute-start(bf16[128,7168]{1,0:T(8,128)(2,1)} %collective-permute-done.5.refs_1_), channel_id=1, source_target_pairs={{0,8},{4,20},{8,0},{12,28},{16,24},{20,4},{24,16},{28,12},{1,9},{5... | collective-permute-start | bytes 5505032 | tf_op jit(solution)/shard_map/ppermute | solution.py:341
  46.3 42.1 %collective-permute-start.14 = (bf16[128,7168]{1,0:T(8,128)(2,1)}, bf16[128,7168]{1,0:T(8,128)(2,1)}, u32[]{:S(2)}, u32[]{:S(2)}) collective-permute-start(bf16[128,7168]{1,0:T(8,128)(2,1)} %collective-permute-done.13.refs_2_), channel_id=1, source_target_pairs={{0,8},{4,20},{8,0},{12,28},{16,24},{20,4},{24,16},{28,12},{1,9},{5... | collective-permute-start | bytes 5505032 | tf_op jit(solution)/shard_map/ppermute | solution.py:341
  49.6 68.9 %collective-permute-start.10 = (bf16[128,7168]{1,0:T(8,128)(2,1)}, bf16[128,7168]{1,0:T(8,128)(2,1)}, u32[]{:S(2)}, u32[]{:S(2)}) collective-permute-start(bf16[128,7168]{1,0:T(8,128)(2,1)} %collective-permute-done.9.refs_2_), channel_id=1, source_target_pairs={{0,8},{4,20},{8,0},{12,28},{16,24},{20,4},{24,16},{28,12},{1,9},{5... | collective-permute-start | bytes 5505032 | tf_op jit(solution)/shard_map/ppermute | solution.py:341
  53.3 64.5 %collective-permute-start.3 = (bf16[64,7168]{1,0:T(8,128)(2,1)S(1)}, bf16[64,7168]{1,0:T(8,128)(2,1)S(1)}, u32[]{:S(2)}, u32[]{:S(2)}) collective-permute-start(bf16[64,7168]{1,0:T(8,128)(2,1)S(1)} %get-tuple-element.149), channel_id=1, source_target_pairs={{0,8},{4,20},{8,0},{12,28},{16,24},{20,4},{24,16},{28,12},{1,9},{5... | collective-permute-start | bytes 2752520 | tf_op jit(solution)/shard_map/ppermute | solution.py:341
  53.7 74.0 %collective-permute-start.1 = (bf16[64,7168]{1,0:T(8,128)(2,1)S(1)}, bf16[64,7168]{1,0:T(8,128)(2,1)S(1)}, u32[]{:S(2)}, u32[]{:S(2)}) collective-permute-start(bf16[64,7168]{1,0:T(8,128)(2,1)S(1)} %get-tuple-element.150), channel_id=1, source_target_pairs={{0,8},{4,20},{8,0},{12,28},{16,24},{20,4},{24,16},{28,12},{1,9},{5... | collective-permute-start | bytes 2752520 | tf_op jit(solution)/shard_map/ppermute | solution.py:341
  88.4 68.2 %collective-permute-start.15 = (bf16[128,7168]{1,0:T(8,128)(2,1)}, bf16[128,7168]{1,0:T(8,128)(2,1)S(1)}, u32[]{:S(2)}, u32[]{:S(2)}) collective-permute-start(bf16[128,7168]{1,0:T(8,128)(2,1)} %collective-permute-done.14.refs_1_), channel_id=1, source_target_pairs={{0,4},{4,0},{8,12},{12,8},{16,20},{20,16},{24,28},{28,24},{1,5},{5... | collective-permute-start | bytes 5505032 | tf_op jit(solution)/shard_map/ppermute | solution.py:338
  118.5 56.3 %collective-permute-start.11 = (bf16[128,7168]{1,0:T(8,128)(2,1)}, bf16[128,7168]{1,0:T(8,128)(2,1)}, u32[]{:S(2)}, u32[]{:S(2)}) collective-permute-start(bf16[128,7168]{1,0:T(8,128)(2,1)} %collective-permute-done.10.refs_1_), channel_id=1, source_target_pairs={{0,4},{4,0},{8,12},{12,8},{16,20},{20,16},{24,28},{28,24},{1,5},{5... | collective-permute-start | bytes 5505032 | tf_op jit(solution)/shard_map/ppermute | solution.py:338
  131.9 83.4 %collective-permute-start.7 = (bf16[128,7168]{1,0:T(8,128)(2,1)}, bf16[128,7168]{1,0:T(8,128)(2,1)S(1)}, u32[]{:S(2)}, u32[]{:S(2)}) collective-permute-start(bf16[128,7168]{1,0:T(8,128)(2,1)} %collective-permute-done.6.refs_1_), channel_id=1, source_target_pairs={{0,4},{4,0},{8,12},{12,8},{16,20},{20,16},{24,28},{28,24},{1,5},{5... | collective-permute-start | bytes 5505032 | tf_op jit(solution)/shard_map/ppermute | solution.py:338
  133.6 51.6 %collective-permute-start.39 = (bf16[2,272,1024]{2,1,0:T(8,128)(2,1)S(1)}, bf16[2,272,1024]{2,1,0:T(8,128)(2,1)S(1)}, u32[]{:S(2)}, u32[]{:S(2)}) collective-permute-start(bf16[2,272,1024]{2,1,0:T(8,128)(2,1)S(1)} %get-tuple-element.129), channel_id=1, source_target_pairs={{3,0},{7,4},{10,9},{14,13},{17,18},{21,22},{24,27},{28,31}} | collective-permute-start | bytes 3342344 | tf_op jit(solution)/shard_map/ppermute | solution.py:349
  154.5 32.1 %collective-permute-start.4 = (bf16[64,7168]{1,0:T(8,128)(2,1)S(1)}, bf16[64,7168]{1,0:T(8,128)(2,1)}, u32[]{:S(2)}, u32[]{:S(2)}) collective-permute-start(bf16[64,7168]{1,0:T(8,128)(2,1)S(1)} %collective-permute-done.3.refs_1_), channel_id=1, source_target_pairs={{0,4},{4,0},{8,12},{12,8},{16,20},{20,16},{24,28},{28,24},{1,5},{5... | collective-permute-start | bytes 2752520 | tf_op jit(solution)/shard_map/ppermute | solution.py:338
  156.7 56.0 %collective-permute-start.2 = (bf16[64,7168]{1,0:T(8,128)(2,1)S(1)}, bf16[64,7168]{1,0:T(8,128)(2,1)}, u32[]{:S(2)}, u32[]{:S(2)}) collective-permute-start(bf16[64,7168]{1,0:T(8,128)(2,1)S(1)} %collective-permute-done.1.refs_1_), channel_id=1, source_target_pairs={{0,4},{4,0},{8,12},{12,8},{16,20},{20,16},{24,28},{28,24},{1,5},{5... | collective-permute-start | bytes 2752520 | tf_op jit(solution)/shard_map/ppermute | solution.py:338
  174.8 39.2 %collective-permute-start.34 = (bf16[1,144,1024]{2,1,0:T(8,128)(2,1)S(1)}, bf16[1,144,1024]{2,1,0:T(8,128)(2,1)S(1)}, u32[]{:S(2)}, u32[]{:S(2)}) collective-permute-start(bf16[1,144,1024]{2,1,0:T(8,128)(2,1)S(1)} %get-tuple-element.122), channel_id=1, source_target_pairs={{0,1},{3,2},{4,5},{7,6},{9,8},{10,11},{13,12},{14,15},{18,19},{17,... | collective-permute-start | bytes 884744 | tf_op jit(solution)/shard_map/ppermute | solution.py:349
  185.2 44.0 %collective-permute-start.35 = (bf16[1,144,1024]{2,1,0:T(8,128)(2,1)S(1)}, bf16[1,144,1024]{2,1,0:T(8,128)(2,1)S(1)}, u32[]{:S(2)}, u32[]{:S(2)}) collective-permute-start(bf16[1,144,1024]{2,1,0:T(8,128)(2,1)S(1)} %get-tuple-element.123), channel_id=1, source_target_pairs={{3,1},{0,2},{7,5},{4,6},{10,8},{9,11},{14,12},{13,15},{17,19},{18,... | collective-permute-start | bytes 884744 | tf_op jit(solution)/shard_map/ppermute | solution.py:349
  186.5 51.2 %collective-permute-start.36 = (bf16[1,144,1024]{2,1,0:T(8,128)(2,1)S(1)}, bf16[1,144,1024]{2,1,0:T(8,128)(2,1)S(1)}, u32[]{:S(2)}, u32[]{:S(2)}) collective-permute-start(bf16[1,144,1024]{2,1,0:T(8,128)(2,1)S(1)} %get-tuple-element.124), channel_id=1, source_target_pairs={{2,1},{1,2},{6,5},{5,6},{11,8},{8,11},{15,12},{12,15},{16,19},{19,... | collective-permute-start | bytes 884744 | tf_op jit(solution)/shard_map/ppermute | solution.py:349
  215.3 55.4 %collective-permute-start.28 = (bf16[2,144,1024]{2,1,0:T(8,128)(2,1)S(1)}, bf16[2,144,1024]{2,1,0:T(8,128)(2,1)S(1)}, u32[]{:S(2)}, u32[]{:S(2)}) collective-permute-start(bf16[2,144,1024]{2,1,0:T(8,128)(2,1)S(1)} %get-tuple-element.112), channel_id=1, source_target_pairs={{2,3},{6,7},{11,10},{15,14},{16,17},{20,21},{25,24},{29,28}} | collective-permute-start | bytes 1769480 | tf_op jit(solution)/shard_map/ppermute | solution.py:349
  237.8 28.8 %collective-permute-start.22 = (bf16[1,144,1024]{2,1,0:T(8,128)(2,1)S(1)}, bf16[1,144,1024]{2,1,0:T(8,128)(2,1)S(1)}, u32[]{:S(2)}, u32[]{:S(2)}) collective-permute-start(bf16[1,144,1024]{2,1,0:T(8,128)(2,1)S(1)} %get-tuple-element.102), channel_id=1, source_target_pairs={{0,1},{3,2},{4,5},{7,6},{9,8},{10,11},{13,12},{14,15},{18,19},{17,... | collective-permute-start | bytes 884744 | tf_op jit(solution)/shard_map/ppermute | solution.py:349
  240.4 29.6 %collective-permute-start.24 = (bf16[1,144,1024]{2,1,0:T(8,128)(2,1)S(1)}, bf16[1,144,1024]{2,1,0:T(8,128)(2,1)S(1)}, u32[]{:S(2)}, u32[]{:S(2)}) collective-permute-start(bf16[1,144,1024]{2,1,0:T(8,128)(2,1)S(1)} %get-tuple-element.104), channel_id=1, source_target_pairs={{2,1},{1,2},{6,5},{5,6},{11,8},{8,11},{15,12},{12,15},{16,19},{19,... | collective-permute-start | bytes 884744 | tf_op jit(solution)/shard_map/ppermute | solution.py:349
  267.3 64.5 %collective-permute-start.25 = (bf16[2,144,1024]{2,1,0:T(8,128)(2,1)S(1)}, bf16[2,144,1024]{2,1,0:T(8,128)(2,1)S(1)}, u32[]{:S(2)}, u32[]{:S(2)}) collective-permute-start(bf16[2,144,1024]{2,1,0:T(8,128)(2,1)S(1)} %get-tuple-element.107), channel_id=1, source_target_pairs={{2,3},{6,7},{11,10},{15,14},{16,17},{20,21},{25,24},{29,28}} | collective-permute-start | bytes 1769480 | tf_op jit(solution)/shard_map/ppermute | solution.py:349
  270.0 63.1 %collective-permute-start.26 = (bf16[2,144,1024]{2,1,0:T(8,128)(2,1)S(1)}, bf16[2,144,1024]{2,1,0:T(8,128)(2,1)S(1)}, u32[]{:S(2)}, u32[]{:S(2)}) collective-permute-start(bf16[2,144,1024]{2,1,0:T(8,128)(2,1)S(1)} %get-tuple-element.108), channel_id=1, source_target_pairs={{1,3},{5,7},{8,10},{12,14},{19,17},{23,21},{26,24},{30,28}} | collective-permute-start | bytes 1769480 | tf_op jit(solution)/shard_map/ppermute | solution.py:349
  270.7 63.7 %collective-permute-start.27 = (bf16[2,144,1024]{2,1,0:T(8,128)(2,1)S(1)}, bf16[2,144,1024]{2,1,0:T(8,128)(2,1)S(1)}, u32[]{:S(2)}, u32[]{:S(2)}) collective-permute-start(bf16[2,144,1024]{2,1,0:T(8,128)(2,1)S(1)} %get-tuple-element.109), channel_id=1, source_target_pairs={{0,3},{4,7},{9,10},{13,14},{18,17},{22,21},{27,24},{31,28}} | collective-permute-start | bytes 1769480 | tf_op jit(solution)/shard_map/ppermute | solution.py:349
  276.2 64.1 %collective-permute-start.20 = (bf16[1,80,1024]{2,1,0:T(8,128)(2,1)S(1)}, bf16[1,80,1024]{2,1,0:T(8,128)(2,1)S(1)}, u32[]{:S(2)}, u32[]{:S(2)}) collective-permute-start(bf16[1,80,1024]{2,1,0:T(8,128)(2,1)S(1)} %get-tuple-element.98), channel_id=1, source_target_pairs={{3,1},{0,2},{7,5},{4,6},{10,8},{9,11},{14,12},{13,15},{17,19},{18,... | collective-permute-start | bytes 491528 | tf_op jit(solution)/shard_map/ppermute | solution.py:349
  277.5 62.8 %collective-permute-start.21 = (bf16[1,80,1024]{2,1,0:T(8,128)(2,1)S(1)}, bf16[1,80,1024]{2,1,0:T(8,128)(2,1)S(1)}, u32[]{:S(2)}, u32[]{:S(2)}) collective-permute-start(bf16[1,80,1024]{2,1,0:T(8,128)(2,1)S(1)} %get-tuple-element.99), channel_id=1, source_target_pairs={{2,1},{1,2},{6,5},{5,6},{11,8},{8,11},{15,12},{12,15},{16,19},{19,... | collective-permute-start | bytes 491528 | tf_op jit(solution)/shard_map/ppermute | solution.py:349
  (31 other events, 656.1 us)
